TPU v7x, 128 devices: a whole 4x4x4 slice. The times are simulated.
128 devices in a mesh: rows: 64 (over x, y_lo, z, core), rep: 2 (over y_hi).
Axes of the slice: x: 4, y: 4 (y_hi: 2, y_lo: 2; y = y_hi * 2 + y_lo), z: 4, core: 2. Of those that a mesh axis runs over, the one named last changes fastest.
Arguments:
- features: bfloat16 [65536, 128], P(('rows', 'rep')), may hold values from -6 to 6
- weight: bfloat16 [128, 256], replicated, may hold values from -0.5 to 0.5
- shift_bias: float32 [256], replicated, may hold values from -3 to 3
- norm_gain: float32 [256], replicated, may hold values from 0.25 to 1.75
- tile_values: bfloat16 [512, 2, 88, 128, 128], P('rows', 'rep'), as said below
- tile_cols: int32 [512, 2, 88], P('rows', 'rep'), may hold values from 0 to 255, all different within a row
- tile_counts: int32 [512, 2], P('rows', 'rep'), may hold values from 1 to 88, as said below
- block_order: int32 [2, 256], replicated, may hold values from 0 to 255, each once within a row
Outputs:
- node_out: bfloat16 [65536, 256], P(('rows', 'rep'))
Inputs may be any that keep to these rules, and one draw needn't show every extreme that they name: Slots 0 to tile_counts - 1 of a row block and column set are live, the rest are ignored; the largest count is reached. `tile_values`: tile entries are nonnegative.
All inputs are finite; a program needn't handle non-finite values.
Results may differ from a plain program's by a relative error of at most 0.0052.
Values may be sent and summed in bfloat16 or wider, within the bound.
No kernel may reach another device: no remote copies, remote signals or barrier semaphores. Data moves between devices by JAX's collectives and lax.ppermute only.
A program may use at most 192 MiB of HBM per device.

v0:
```python
import jax
import jax.numpy as jnp
from jax import lax
from jax.sharding import PartitionSpec as P


def per_device(
    features, weight, shift_bias, norm_gain, tile_values, tile_cols, tile_counts, block_order
):
    row_blocks = tile_values.shape[0]
    slot_count = tile_values.shape[2]
    block_size = tile_values.shape[3]
    hidden_width = weight.shape[1]
    projected = jnp.dot(features, weight, preferred_element_type=jnp.float32).astype(jnp.bfloat16)
    panel_rows = lax.all_gather(projected, "rows", axis=0, tiled=True)
    set_blocks = panel_rows.shape[0] // block_size
    panel_blocks = panel_rows.reshape(set_blocks, block_size, hidden_width)
    order_mine = lax.dynamic_index_in_dim(block_order, lax.axis_index("rep"), 0, keepdims=False)
    column_ids = tile_cols.reshape(row_blocks, slot_count)
    matches = column_ids[:, :, None] == jnp.arange(set_blocks, dtype=jnp.int32)[None, None, :]
    positions = jnp.sum(jnp.where(matches, order_mine[None, None, :], 0), axis=2)
    tile_block = tile_values.reshape(row_blocks, slot_count, block_size, block_size)
    live_count = tile_counts.reshape(row_blocks)
    picked_rows = panel_blocks[positions]
    live_mask = jnp.arange(slot_count, dtype=jnp.int32)[None, :] < live_count[:, None]
    picked_rows = jnp.where(live_mask[:, :, None, None], picked_rows, jnp.zeros((), jnp.bfloat16))
    summed = jnp.einsum(
        "bkij,bkjh->bih", tile_block, picked_rows, preferred_element_type=jnp.float32
    )
    row_half = lax.psum_scatter(
        summed.reshape(row_blocks * block_size, hidden_width),
        "rep",
        scatter_dimension=0,
        tiled=True,
    )
    hidden = jnp.maximum(row_half + shift_bias, 0.0)
    row_mean = jnp.mean(hidden, axis=1, keepdims=True)
    centered = hidden - row_mean
    row_var = jnp.mean(centered * centered, axis=1, keepdims=True)
    return (centered / jnp.sqrt(row_var + 1e-05) * norm_gain).astype(jnp.bfloat16)


def solution(mesh):
    in_specs = (
        P(("rows", "rep"), None),
        P(),
        P(),
        P(),
        P("rows", "rep", None, None, None),
        P("rows", "rep", None),
        P("rows", "rep"),
        P(),
    )
    out_specs = P(("rows", "rep"), None)
    return jax.shard_map(
        per_device, mesh=mesh, in_specs=in_specs, out_specs=out_specs, check_vma=False
    )
```

profile of v0, /device:TPU:1, one launch (start us, length us, event | category | flops | bytes accessed | tf_op | source)
XLA Modules:
  0.0 219.7 jit_solution(15019068501015475521)
XLA Ops:
  6.5 0.0 copy-start
  6.5 0.0 all-gather.2.cloned.1.call-start
  6.5 0.9 copy-done
  7.4 1.8 convolution_convert_fusion
  9.2 0.0 all-gather.2.cloned.1.call-update
  9.2 0.0 reduce-scatter.2.cloned.1.call-start
  9.3 0.7 constant_dynamic-slice_fusion
  10.0 1.0 select_reduce_fusion
  11.0 0.1 reshape.66
  11.1 0.7 iota_compare_fusion.1
  11.8 123.1 %all-gather.2.cloned.1.call-done = bf16[32768,256]{1,0:T(8,128)(2,1)} async-done(((bf16[512,256]{1,0:T(8,128)(2,1)}), bf16[32768,256]{1,0:T(8,128)(2,1)}) %all-gather.2.cloned.1.call-update) | async-done | bytes 16777232 | tf_op jit(solution)/shard_map/all_gather | solution.py:15
  134.9 26.7 %gather_fusion = bf16[704,128,256]{2,1,0:T(8,128)(2,1)} fusion(bf16[256,128,256]{2,1,0:T(8,128)(2,1)} %bitcast.20, s32[1024]{0:T(1024)S(1)} %pad_clamp_fusion), kind=kCustom, calls=%fused_computation | custom fusion | bytes 92277504 | tf_op jit(solution)/shard_map/gather | solution.py:24
  161.6 0.0 copy-start.1
  161.6 0.0 copy-start.2
  161.6 0.0 copy-start.3
  161.6 23.8 %fusion = f32[8,256,128,1]{1,2,3,0:T(8,128)} fusion(bf16[8,88,128,256]{3,2,1,0:T(8,128)(2,1)} %bitcast.21, pred[8,88]{1,0:T(8,128)(4,1)S(1)} %iota_compare_fusion.1, bf16[8,1,88,128,128]{4,3,2,1,0:T(8,128)(2,1)} %param.12), kind=kOutput, calls=%fused_computation.1 | convolution fusion | flops 5928648704 | bytes 70255296 | tf_op jit(solution)/shard_map/bkij,bkjh->bih/dot_general | solution.py:27
  185.4 0.0 reduce-scatter.2.cloned.1.call-update
  185.4 23.0 %reduce-scatter.2.cloned.1.call-done = f32[512,256]{1,0:T(8,128)} async-done(((f32[1024,256]{1,0:T(8,128)}), f32[512,256]{1,0:T(8,128)}) %reduce-scatter.2.cloned.1.call-update) | async-done | bytes 524304 | tf_op jit(solution)/shard_map/reduce_scatter | solution.py:30
  208.4 0.0 copy-done.2
  208.4 1.2 fusion.5
  209.6 1.3 multiply_reduce_fusion
  210.9 0.0 copy-done.3
  210.9 2.0 multiply_convert_fusion
  212.9 0.0 copy-done.1
  (4 shorter events, 0.0 us)
Async XLA Ops:
  6.5 0.9 copy-start
  6.5 128.4 %all-gather.2.cloned.1.call-start = ((), (), s32[]{:S(2)}) async-start(), calls=%async_computation.1 | async-start | bytes 17039360 | tf_op jit(solution)/shard_map/all_gather | solution.py:15
  9.2 199.2 %reduce-scatter.2.cloned.1.call-start = ((), (), s32[]{:S(2)}) async-start(), calls=%async_computation.2 | async-start | bytes 1572864 | tf_op jit(solution)/shard_map/reduce_scatter | solution.py:30
  161.6 51.2 %copy-start.1 = (bf16[512,128]{1,0:T(8,128)(2,1)S(1)}, bf16[512,128]{1,0:T(8,128)(2,1)}, u32[]{:S(2)}) copy-start(bf16[512,128]{1,0:T(8,128)(2,1)} %param.8) | copy-start | bytes 393220
  161.6 46.8 %copy-start.2 = (f32[256]{0:T(256)S(1)}, f32[256]{0:T(256)}, u32[]{:S(2)}) copy-start(f32[256]{0:T(256)} %param.10) | copy-start | bytes 3076
  161.6 49.3 %copy-start.3 = (f32[256]{0:T(256)S(1)}, f32[256]{0:T(256)}, u32[]{:S(2)}) copy-start(f32[256]{0:T(256)} %param.11) | copy-start | bytes 3076
Sparse Core Ops, SparseCore 0:
  9.3 125.5 all-gather.1
  185.6 22.8 reduce-scatter.1
where the time goes:
time: 220 us
  waiting for transfers between devices  146 us (66%)
  local copies, waits for them, and re-layouts  28.4 us (13%)
  matrix products  25.5 us (12%)
  between operations  13.5 us (6%)
  other arithmetic  6.19 us (3%)
    all_gather x1, waiting for transfers between devices, per_device(): panel_rows = lax.all_gather(projected, 'rows', axis=0, tiled=True)  123 us
    gather x1, local copies, waits for them, and re-layouts, per_device(): picked_rows = panel_blocks[positions]  26.7 us
    dot_general x1, matrix products, per_device(): jnp.einsum('bkij,bkjh->bih', tile_block, picked_rows, preferred_element_t...  23.8 us
    reduce_scatter x1, waiting for transfers between devices, per_device(): lax.psum_scatter(summed.reshape(row_blocks * block_size, hidden_width), '...  23 us
  transfers between devices with their start and end apart: 2, of which 2 were waited for; matrix products, arithmetic and copies ran while one was open for 1% of the time, Pallas kernels for 0%

commit v1 on v0

--- a/solution.py
+++ b/solution.py
@@ -12,7 +12,9 @@
     block_size = tile_values.shape[3]
     hidden_width = weight.shape[1]
     projected = jnp.dot(features, weight, preferred_element_type=jnp.float32).astype(jnp.bfloat16)
-    panel_rows = lax.all_gather(projected, "rows", axis=0, tiled=True)
+    panel_rows = jnp.concatenate(
+        lax.all_to_all(jnp.stack([projected] * lax.axis_size("rows")), "rows", 0, 0), axis=0
+    )
     set_blocks = panel_rows.shape[0] // block_size
     panel_blocks = panel_rows.reshape(set_blocks, block_size, hidden_width)
     order_mine = lax.dynamic_index_in_dim(block_order, lax.axis_index("rep"), 0, keepdims=False)

time: 220 us -> 339 us (1.54)
  waiting for transfers between devices: 146 us -> 250 us
  starting transfers between devices: 0.04 us -> 11.1 us
  local copies, waits for them, and re-layouts: 28.4 us -> 33.8 us
    all_to_all x0 -> x1, waiting for transfers between devices: none -> 216 us  [per_device(): lax.all_to_all(jnp.stack([projected] * lax.axis_size('rows')), 'rows', 0, 0)]
    all_gather x1 -> x0, waiting for transfers between devices: 123 us -> none  [per_device(): panel_rows = lax.all_gather(projected, 'rows', axis=0, tiled=True)]
    reduce_scatter x1, waiting for transfers between devices: 23 us -> 34.2 us  [per_device(): lax.psum_scatter(summed.reshape(row_blocks * block_size, hidden_width), '...]
    all_to_all x0 -> x1, starting transfers between devices: none -> 11 us  [per_device(): lax.all_to_all(jnp.stack([projected] * lax.axis_size('rows')), 'rows', 0, 0)]
    another operation x0 -> x1, local copies, waits for them, and re-layouts: none -> 6.05 us  [per_device(): jnp.stack([projected] * lax.axis_size('rows'))]
  transfers between devices with their start and end apart: 2 -> 2, of which waited for: 2 -> 2; matrix products, arithmetic and copies ran while one was open for 1% -> 0% of each run, Pallas kernels for 0% -> 0%
where the time goes in v1:
time: 339 us; the launch traced here: 338 us
  waiting for transfers between devices  250 us (74%)
  local copies, waits for them, and re-layouts  33.8 us (10%)
  matrix products  24.8 us (7%)
  between operations  13.5 us (4%)
  starting transfers between devices  11.1 us (3%)
  other arithmetic  4.85 us (1%)
    all_to_all x1, waiting for transfers between devices, per_device(): lax.all_to_all(jnp.stack([projected] * lax.axis_size('rows')), 'rows', 0, 0)  216 us
    reduce_scatter x1, waiting for transfers between devices, per_device(): lax.psum_scatter(summed.reshape(row_blocks * block_size, hidden_width), '...  34.2 us
    gather x1, local copies, waits for them, and re-layouts, per_device(): picked_rows = panel_blocks[positions]  26.7 us
    dot_general x1, matrix products, per_device(): jnp.einsum('bkij,bkjh->bih', tile_block, picked_rows, preferred_element_t...  23.8 us
    all_to_all x1, starting transfers between devices, per_device(): lax.all_to_all(jnp.stack([projected] * lax.axis_size('rows')), 'rows', 0, 0)  11 us
  transfers between devices with their start and end apart: 2, of which 2 were waited for; matrix products, arithmetic and copies ran while one was open for 0% of the time, Pallas kernels for 0%

profile of v1, /device:TPU:1, one launch (start us, length us, event | category | flops | bytes accessed | tf_op | source)
XLA Modules:
  0.0 338.3 jit_solution(6513841473250034604)
XLA Ops:
  6.5 0.0 copy-start
  6.5 0.0 copy-start.5
  6.5 0.0 copy-start.3
  6.5 0.0 copy-start.6
  6.5 0.9 copy-done
  7.4 1.0 convolution_convert_fusion
  8.5 6.1 %stack.2 = bf16[64,512,256]{2,1,0:T(8,128)(2,1)} broadcast(bf16[512,256]{1,0:T(8,128)(2,1)S(1)} %convolution_convert_fusion), dimensions={1,2} | broadcast | bytes 17039360 | tf_op jit(solution)/shard_map/stack | solution.py:16
  14.5 11.0 %all-to-all-start = ((bf16[64,512,256]{2,1,0:T(8,128)(2,1)}), bf16[64,512,256]{2,1,0:T(8,128)(2,1)}, u32[]{:S(2)}, u32[]{:S(2)}) async-start(bf16[64,512,256]{2,1,0:T(8,128)(2,1)} %stack.2), calls=%async_computation | async-start | bytes 33554432 | tf_op jit(solution)/shard_map/all_to_all | solution.py:16
  25.6 0.0 reduce-scatter.2.cloned.1.call-start
  25.6 0.0 copy-done.5
  25.6 0.0 copy-done.3
  25.7 0.3 select_reduce_fusion
  26.0 0.1 reshape.64
  26.1 0.0 copy-done.6
  26.1 0.1 iota_compare_fusion.1
  26.2 216.1 %all-to-all-done = bf16[64,512,256]{2,1,0:T(8,128)(2,1)} async-done(((bf16[64,512,256]{2,1,0:T(8,128)(2,1)}), bf16[64,512,256]{2,1,0:T(8,128)(2,1)}, u32[]{:S(2)}, u32[]{:S(2)}) %all-to-all-start) | async-done | bytes 16777248 | tf_op jit(solution)/shard_map/all_to_all | solution.py:16
  242.3 26.7 %gather_fusion = bf16[704,128,256]{2,1,0:T(8,128)(2,1)} fusion(bf16[256,128,256]{2,1,0:T(8,128)(2,1)} %bitcast.1, s32[1024]{0:T(1024)S(1)} %pad_clamp_fusion), kind=kCustom, calls=%fused_computation | custom fusion | bytes 92277504 | tf_op jit(solution)/shard_map/gather | solution.py:26
  269.0 0.0 copy-start.1
  269.0 0.0 copy-start.2
  269.0 0.0 copy-start.4
  269.0 23.8 %fusion = f32[8,256,128,1]{1,2,3,0:T(8,128)} fusion(bf16[8,88,128,256]{3,2,1,0:T(8,128)(2,1)} %bitcast.20, pred[8,88]{1,0:T(8,128)(4,1)S(1)} %iota_compare_fusion.1, bf16[8,1,88,128,128]{4,3,2,1,0:T(8,128)(2,1)} %param.12), kind=kOutput, calls=%fused_computation.1 | convolution fusion | flops 5928648704 | bytes 70255296 | tf_op jit(solution)/shard_map/bkij,bkjh->bih/dot_general | solution.py:29
  292.8 0.0 reduce-scatter.2.cloned.1.call-update
  292.8 34.2 %reduce-scatter.2.cloned.1.call-done = f32[512,256]{1,0:T(8,128)} async-done(((f32[1024,256]{1,0:T(8,128)}), f32[512,256]{1,0:T(8,128)}) %reduce-scatter.2.cloned.1.call-update) | async-done | bytes 524304 | tf_op jit(solution)/shard_map/reduce_scatter | solution.py:32
  327.0 0.0 copy-done.2
  327.0 1.2 fusion.5
  328.2 1.3 multiply_reduce_fusion
  329.5 0.0 copy-done.4
  329.5 2.0 multiply_convert_fusion
  331.5 0.0 copy-done.1
  (5 shorter events, 0.0 us)
Async XLA Ops:
  6.5 0.9 copy-start
  6.5 19.1 %copy-start.5 = (s32[2,256]{1,0:T(2,128)S(1)}, s32[2,256]{1,0:T(2,128)}, u32[]{:S(2)}) copy-start(s32[2,256]{1,0:T(2,128)} %param.15) | copy-start | bytes 6148
  6.5 19.1 %copy-start.3 = (s32[8,1,88]{2,1,0:T(1,128)S(1)}, s32[8,1,88]{2,1,0:T(1,128)}, u32[]{:S(2)}) copy-start(s32[8,1,88]{2,1,0:T(1,128)} %param.13) | copy-start | bytes 8452
  6.5 19.6 %copy-start.6 = (s32[8,1]{0,1:T(1,128)S(1)}, s32[8,1]{0,1:T(1,128)}, u32[]{:S(2)}) copy-start(s32[8,1]{0,1:T(1,128)} %param.14) | copy-start | bytes 100
  14.5 227.7 %all-to-all-start = ((bf16[64,512,256]{2,1,0:T(8,128)(2,1)}), bf16[64,512,256]{2,1,0:T(8,128)(2,1)}, u32[]{:S(2)}, u32[]{:S(2)}) async-start(bf16[64,512,256]{2,1,0:T(8,128)(2,1)} %stack.2), calls=%async_computation | async-start | bytes 33554432 | tf_op jit(solution)/shard_map/all_to_all | solution.py:16
  25.6 301.4 %reduce-scatter.2.cloned.1.call-start = ((), (), s32[]{:S(2)}) async-start(), calls=%async_computation.2 | async-start | bytes 1572864 | tf_op jit(solution)/shard_map/reduce_scatter | solution.py:32
  269.0 62.5 %copy-start.1 = (bf16[512,128]{1,0:T(8,128)(2,1)S(1)}, bf16[512,128]{1,0:T(8,128)(2,1)}, u32[]{:S(2)}) copy-start(bf16[512,128]{1,0:T(8,128)(2,1)} %param.8) | copy-start | bytes 393220
  269.0 58.0 %copy-start.2 = (f32[256]{0:T(256)S(1)}, f32[256]{0:T(256)}, u32[]{:S(2)}) copy-start(f32[256]{0:T(256)} %param.10) | copy-start | bytes 3076
  269.0 60.5 %copy-start.4 = (f32[256]{0:T(256)S(1)}, f32[256]{0:T(256)}, u32[]{:S(2)}) copy-start(f32[256]{0:T(256)} %param.11) | copy-start | bytes 3076
Sparse Core Ops, SparseCore 0:
  292.9 34.0 reduce-scatter.1
